TPU v7x, 32 devices: a whole 2x2x4 slice. The times are simulated.
32 devices in a mesh: cfg: 1, pair: 16 (over z, y, x), blk: 2 (over core).
Axes of the slice: x: 2, y: 2, z: 4, core: 2. Of those that a mesh axis runs over, the one named last changes fastest.
Arguments:
- elementals: bfloat16 [16, 8, 2, 65536], P('cfg', None, None, ('pair', 'blk')), may hold values from -0.079589844 to 0.079589844
- perambulator: bfloat16 [16, 2, 1024, 1024], P(('cfg', 'pair'), None, None, 'blk'), may hold values from -0.1875 to 0.1875
- pairs: int32 [16, 2], replicated, may hold values from 0 to 15, as said below
- elem_index: int32 [16, 24], replicated, may hold values from 0 to 7
- coef_code: int32 [16, 24, 4, 4], replicated, may hold values from -2 to 2
- term_count: int32 [16], replicated, may hold values from 12 to 24, as said below
Outputs:
- correlator: float32 [16, 2], P(('cfg', 'pair'))
Inputs may be any that keep to these rules, and one draw needn't show every extreme that they name: `pairs`: pair p + 8 lists the two timeslices of pair p in reverse order; the two timeslices of a pair differ. `term_count`: some pair uses all 24 terms.
All inputs are finite; a program needn't handle non-finite values.
Results may differ from a plain program's by a relative error of at most 0.0057.
Values may be sent and summed in bfloat16 or wider, within the bound.
No kernel may reach another device: no remote copies, remote signals or barrier semaphores. Data moves between devices by JAX's collectives and lax.ppermute only.
A program may use at most 64 MiB of HBM per device.

v0:
```python
import jax
import jax.numpy as jnp
from jax import lax
from jax.sharding import PartitionSpec as P

NV = 256
NS = 4


def partner(value, axis, apart):
    return lax.ppermute(value, axis, [(i, i ^ 1 << apart) for i in range(lax.axis_size(axis))])


def shards(elementals, perambulator, pairs, elem_index, coef_code, term_count):
    peers = lax.axis_size("pair")
    entries = elementals.shape[-1]
    nterms = elem_index.shape[1]
    used = (jnp.arange(nterms)[None, :] < term_count[:, None]).astype(jnp.float32)
    weights = (coef_code.astype(jnp.float32) * 0.5 * used[:, :, None, None]).astype(jnp.bfloat16)
    picked = elementals[pairs[:, 0][:, None], elem_index]
    combined = jnp.einsum(
        "pkab,pkcf->pabcf", weights, picked, preferred_element_type=jnp.float32
    ).astype(jnp.bfloat16)
    blocks = lax.all_to_all(combined, "pair", split_axis=0, concat_axis=0, tiled=True)
    gathered = lax.all_gather(blocks[:, None], "blk", axis=1, tiled=True)
    propagator = perambulator[0]
    columns = propagator.shape[-1]
    shaped = gathered.reshape(2 * peers, NS, NS, 2, entries // NV, NV)
    phi_real = shaped[:, :, :, 0]
    phi_imag = shaped[:, :, :, 1]
    prop_real = propagator[0].reshape(NS, NV, columns)
    prop_imag = propagator[1].reshape(NS, NV, columns)
    form = "gabuj,bjn->agun"
    dressed_real = jnp.einsum(
        form, phi_real, prop_real, preferred_element_type=jnp.float32
    ) - jnp.einsum(form, phi_imag, prop_imag, preferred_element_type=jnp.float32)
    dressed_imag = jnp.einsum(
        form, phi_real, prop_imag, preferred_element_type=jnp.float32
    ) + jnp.einsum(form, phi_imag, prop_real, preferred_element_type=jnp.float32)
    dressed = (
        jnp.stack([dressed_real, dressed_imag]).astype(jnp.bfloat16).reshape(2, NS * NV, columns)
    )
    mirror_bit = peers.bit_length() - 2
    mirror = partner(dressed, "pair", mirror_bit)
    mirror_rows = lax.all_to_all(mirror, "blk", split_axis=1, concat_axis=2, tiled=True)
    products = jnp.einsum("zrc,ycr->zy", dressed, mirror_rows, preferred_element_type=jnp.float32)
    partial_trace = jnp.stack([products[0, 0] - products[1, 1], products[0, 1] + products[1, 0]])
    total = lax.psum(partial_trace, "blk")
    return total[None, :]


def solution(mesh):
    return jax.shard_map(
        shards,
        mesh=mesh,
        in_specs=(
            P("cfg", None, None, ("pair", "blk")),
            P(("cfg", "pair"), None, None, "blk"),
            P(),
            P(),
            P(),
            P(),
        ),
        out_specs=P(("cfg", "pair"), None),
        check_vma=False,
    )
```

profile of v0, /device:TPU:0, one launch (start us, length us, event | category | flops | bytes accessed | tf_op | source)
XLA Modules:
  0.0 274.8 jit_solution(7903193112295483595)
XLA Ops:
  8.9 19.0 %gather_fusion = bf16[384,2,2048]{2,1,0:T(2,128)(2,1)} fusion(bf16[16,8,2,2048]{3,2,1,0:T(2,128)(2,1)S(1)} %copy-done, s32[384]{0:T(512)S(1)} %reshape.44), kind=kCustom, calls=%fused_computation | custom fusion | bytes 6294528 | tf_op jit(solution)/shard_map/gather | solution.py:20
  28.0 4.5 %fusion.2 = bf16[16,4,4,2,2048]{4,2,3,1,0:T(4,128)(2,1)S(1)} fusion(bf16[16,24,2,2048,1]{3,2,1,0,4:T(2,128)(2,1)} %bitcast.96, s32[16,24,4,4]{1,3,2,0:T(4,128)S(1)} %copy-done.6, f32[16,24]{1,0:T(8,128)S(1)} %fusion.20), kind=kOutput, calls=%fused_computation.3 | convolution fusion | flops 51398656 | bytes 5268992 | tf_op jit(solution)/shard_map/pkab,pkcf->pabcf/dot_general | solution.py:21
  32.5 57.0 %all_to_all.23 = bf16[16,4,4,2,2048]{4,2,3,1,0:T(4,128)(2,1)} all-to-all(bf16[16,4,4,2,2048]{4,2,3,1,0:T(4,128)(2,1)S(1)} %fusion.2), channel_id=1, replica_groups=mesh['cfg'=1,'pair'=16,'blk'=2] {'pair'}, dimensions={0} | all-to-all | bytes 4194304 | tf_op jit(solution)/shard_map/all_to_all | solution.py:24
  89.5 1.6 copy-done.3
  91.1 1.5 fusion.24
  92.6 9.1 %all-gather.3.cloned.1.call-done = bf16[16,8,4,2,2048]{4,2,3,1,0:T(4,128)(2,1)} async-done(((bf16[16,4,4,2,2048]{4,2,3,1,0:T(4,128)(2,1)}), bf16[16,8,4,2,2048]{4,2,3,1,0:T(4,128)(2,1)}) %all-gather.3.cloned.1.call-update) | async-done | bytes 4194320 | tf_op jit(solution)/shard_map/all_gather | solution.py:25
  101.7 7.7 %reshape.43 = bf16[32,4,4,2,8,256]{5,4,2,3,1,0:T(8,128)(2,1)} reshape(bf16[16,8,4,2,2048]{4,2,3,1,0:T(4,128)(2,1)} %all-gather.3.cloned.1.call-done) | data formatting | bytes 8388608 | tf_op jit(solution)/shard_map/reshape | solution.py:28
  109.4 3.0 %fusion.7 = f32[32,4,8,512,1]{3,2,4,1,0:T(8,128)S(1)} fusion(bf16[4,256,512,1,1]{2,1,0,4,3:T(8,128)(2,1)S(1)} %bitcast.102, bf16[32,4,4,2,8,256]{5,4,2,3,1,0:T(8,128)(2,1)} %reshape.43), kind=kOutput, calls=%fused_computation.12 | convolution fusion | flops 1073741824 | bytes 5242880 | tf_op jit(solution)/shard_map/gabuj,bjn->agun/dot_general | solution.py:37
  112.5 2.6 fusion.8
  115.1 1.3 fusion.12
  116.3 1.1 copy.32
  117.4 4.7 %copy.34 = bf16[1,1024,512]{1,0,2:T(2,128)(2,1)S(1)} copy(bf16[1,1024,512]{2,1,0:T(8,128)(2,1)} %bitcast.99) | data formatting | bytes 2097152 | tf_op jit(solution)/shard_map/stack | solution.py:41
  122.2 3.8 %fusion.11 = bf16[4,32,8,512]{3,2,0,1:T(8,128)(2,1)S(1)} fusion(bf16[4,256,512,1,1]{2,1,0,4,3:T(8,128)(2,1)} %bitcast.101, bf16[32,4,4,2,8,256]{5,4,2,3,1,0:T(8,128)(2,1)} %reshape.43, f32[32,4,8,512,1]{3,2,4,1,0:T(8,128)} %fusion.8), kind=kOutput, calls=%fused_computation.16 | convolution fusion | flops 1074790400 | bytes 6291456 | tf_op jit(solution)/shard_map/gabuj,bjn->agun/dot_general | solution.py:36
  126.0 1.1 copy.31
  127.1 6.0 %copy.33 = bf16[1,1024,512]{1,0,2:T(2,128)(2,1)} copy(bf16[1,1024,512]{2,1,0:T(8,128)(2,1)} %bitcast.100) | data formatting | bytes 2097152 | tf_op jit(solution)/shard_map/stack | solution.py:41
  133.0 5.9 %pad_maximum_fusion = bf16[2,1024,512]{1,0,2:T(2,128)(2,1)S(1)} fusion(bf16[1,1024,512]{1,0,2:T(2,128)(2,1)S(1)} %copy.34, bf16[1,1024,512]{1,0,2:T(2,128)(2,1)} %copy.33), kind=kLoop, calls=%fused_computation.6 | loop fusion | flops 4194304 | bytes 4194304 | tf_op jit(solution)/shard_map/stack | solution.py:41
  138.9 2.7 collective-permute-start
  141.7 91.1 %collective-permute-done = bf16[2,1024,512]{1,0,2:T(2,128)(2,1)} collective-permute-done((bf16[2,1024,512]{1,0,2:T(2,128)(2,1)S(1)}, bf16[2,1024,512]{1,0,2:T(2,128)(2,1)}, u32[]{:S(2)}, u32[]{:S(2)}) %collective-permute-start) | collective-permute-done | bytes 2097184 | tf_op jit(solution)/shard_map/ppermute | solution.py:11
  232.8 8.3 %copy.35 = bf16[2,1024,512]{2,0,1:T(2,128)(2,1)S(1)} copy(bf16[2,1024,512]{1,0,2:T(2,128)(2,1)} %collective-permute-done) | data formatting | bytes 4194304 | tf_op jit(solution)/shard_map/ppermute | solution.py:11
  241.1 5.4 %all_to_all.24 = bf16[2,1024,512]{2,0,1:T(2,128)(2,1)S(1)} all-to-all(bf16[2,1024,512]{2,0,1:T(2,128)(2,1)S(1)} %copy.35), channel_id=1, replica_groups=mesh['cfg'=1,'pair'=16,'blk'=2] {'blk'}, dimensions={1} | all-to-all | bytes 4194304 | tf_op jit(solution)/shard_map/all_to_all | solution.py:45
  246.5 3.2 %copy.54 = bf16[2,2,512,512]{3,1,0,2:T(2,128)(2,1)S(1)} copy(bf16[2,2,512,512]{3,0,2,1:T(2,128)(2,1)S(1)} %bitcast.97) | data formatting | bytes 4194304 | tf_op jit(solution)/shard_map/all_to_all | solution.py:45
  249.8 2.6 all_to_all.20
  252.4 9.3 %convolution_bitcast_fusion = f32[2,2]{1,0:T(2,128)S(1)} fusion(bf16[2,1024,512]{1,0,2:T(2,128)(2,1)} %copy-done.2, bf16[2,512,1024]{2,0,1:T(2,128)(2,1)} %all_to_all.20), kind=kOutput, calls=%fused_computation.18 | convolution fusion | flops 4194304 | bytes 4194320 | tf_op jit(solution)/shard_map/zrc,ycr->zy/dot_general | solution.py:46
  265.0 2.9 %psum.7 = f32[1,2]{1,0:T(1,128)} all-reduce(f32[1,2]{1,0:T(1,128)S(1)} %maximum_bitcast_fusion), channel_id=1, replica_groups=mesh['cfg'=1,'pair'=16,'blk'=2] {'blk'}, use_global_device_ids=true, to_apply=%region_0.0 | all-reduce | flops 2 | bytes 16 | tf_op jit(solution)/shard_map/psum | solution.py:48
  (21 shorter events, 3.2 us)
Async XLA Ops:
  6.5 2.4 copy-start
  6.5 95.2 %all-gather.3.cloned.1.call-start = ((), (), s32[]{:S(2)}) async-start(), calls=%async_computation.2 | async-start | bytes 6291456 | tf_op jit(solution)/shard_map/all_gather | solution.py:25
  8.9 19.1 %copy-start.6 = (s32[16,24,4,4]{1,3,2,0:T(4,128)S(1)}, s32[16,24,4,4]{1,3,2,0:T(4,128)}, u32[]{:S(2)}) copy-start(s32[16,24,4,4]{1,3,2,0:T(4,128)} %param.10) | copy-start | bytes 73732
  89.5 1.6 copy-start.3
  92.6 16.8 %copy-start.4 = (bf16[1,1,1024,512]{3,2,1,0:T(8,128)(2,1)S(1)}, bf16[1,1,1024,512]{3,2,1,0:T(8,128)(2,1)}, u32[]{:S(2)}) copy-start(bf16[1,1,1024,512]{3,2,1,0:T(8,128)(2,1)} %get-tuple-element.5) | copy-start | bytes 3145732
  109.4 3.0 %copy-start.1 = (bf16[32,4,4,2,8,256]{5,4,2,3,1,0:T(8,128)(2,1)S(1)}, bf16[32,4,4,2,8,256]{5,4,2,3,1,0:T(8,128)(2,1)}, u32[]{:S(2)}) copy-start(bf16[32,4,4,2,8,256]{5,4,2,3,1,0:T(8,128)(2,1)} %reshape.43) | copy-start | bytes 12582916
  109.4 3.1 %copy-start.5 = (bf16[1,1,1024,512]{3,2,1,0:T(8,128)(2,1)S(1)}, bf16[1,1,1024,512]{3,2,1,0:T(8,128)(2,1)}, u32[]{:S(2)}) copy-start(bf16[1,1,1024,512]{3,2,1,0:T(8,128)(2,1)} %get-tuple-element.6) | copy-start | bytes 3145732
  138.9 2.8 %copy-start.2 = (bf16[2,1024,512]{1,0,2:T(2,128)(2,1)}, bf16[2,1024,512]{1,0,2:T(2,128)(2,1)S(1)}, u32[]{:S(2)}) copy-start(bf16[2,1024,512]{1,0,2:T(2,128)(2,1)S(1)} %pad_maximum_fusion) | copy-start | bytes 6291460
  138.9 93.9 %collective-permute-start = (bf16[2,1024,512]{1,0,2:T(2,128)(2,1)S(1)}, bf16[2,1024,512]{1,0,2:T(2,128)(2,1)}, u32[]{:S(2)}, u32[]{:S(2)}) collective-permute-start(bf16[2,1024,512]{1,0,2:T(2,128)(2,1)S(1)} %pad_maximum_fusion), channel_id=1, source_target_pairs={{0,16},{2,18},{4,20},{6,22},{8,24},{10,26},{12,28},{14,30},{16,0},... | collective-permute-start | bytes 6291464 | tf_op jit(solution)/shard_map/ppermute | solution.py:11
Sparse Core Ops, SparseCore 0:
  89.7 11.9 all-gather.2
where the time goes:
time: 276 us; the launch traced here: 275 us
  waiting for transfers between devices  100 us (36%)
  blocking collectives  65.4 us (24%)
  local copies, waits for them, and re-layouts  57.7 us (21%)
  matrix products  24.4 us (9%)
  between operations  16 us (6%)
  other arithmetic  8.21 us (3%)
    ppermute x1, waiting for transfers between devices, partner(): lax.ppermute(value, axis, [(i, i ^ 1 << apart) for i in range(lax.axis_si...  91.1 us
    all_to_all x1, blocking collectives, shards(): lax.all_to_all(combined, 'pair', split_axis=0, concat_axis=0, tiled=True)  57 us
    gather x1, local copies, waits for them, and re-layouts, shards(): picked = elementals[pairs[:, 0][:, None], elem_index]  19 us
    another operation x2, local copies, waits for them, and re-layouts, shards(): jnp.stack([dressed_real, dressed_imag]).astype(jnp.bfloat16)  10.7 us
    dot_general x1, matrix products, shards(): jnp.einsum('zrc,ycr->zy', dressed, mirror_rows, preferred_element_type=jn...  9.3 us
    all_gather x1, waiting for transfers between devices, shards(): gathered = lax.all_gather(blocks[:, None], 'blk', axis=1, tiled=True)  9.09 us
    ppermute x1, local copies, waits for them, and re-layouts, partner(): lax.ppermute(value, axis, [(i, i ^ 1 << apart) for i in range(lax.axis_si...  8.31 us
    reshape x1, local copies, waits for them, and re-layouts, shards(): shaped = gathered.reshape(2 * peers, NS, NS, 2, entries // NV, NV)  7.7 us
  transfers between devices with their start and end apart: 2, of which 2 were waited for; matrix products, arithmetic and copies ran while one was open for 1% of the time, Pallas kernels for 0%

commit v1 on v0

--- a/solution.py
+++ b/solution.py
@@ -42,7 +42,15 @@
     )
     mirror_bit = peers.bit_length() - 2
     mirror = partner(dressed, "pair", mirror_bit)
-    mirror_rows = lax.all_to_all(mirror, "blk", split_axis=1, concat_axis=2, tiled=True)
+    mirror_rows = jnp.concatenate(
+        lax.all_to_all(
+            jnp.stack(jnp.split(mirror, lax.psum(1, axis_name="blk"), axis=1), axis=0),
+            axis_name="blk",
+            split_axis=0,
+            concat_axis=0,
+        ),
+        axis=2,
+    )
     products = jnp.einsum("zrc,ycr->zy", dressed, mirror_rows, preferred_element_type=jnp.float32)
     partial_trace = jnp.stack([products[0, 0] - products[1, 1], products[0, 1] + products[1, 0]])
     total = lax.psum(partial_trace, "blk")

time: 276 us -> 272 us (0.986)
  local copies, waits for them, and re-layouts: 57.7 us -> 51.6 us
  other arithmetic: 8.21 us -> 11.2 us
    ppermute x1 -> x0, local copies, waits for them, and re-layouts: 8.31 us -> none  [partner(): lax.ppermute(value, axis, [(i, i ^ 1 << apart) for i in range(lax.axis_si...]
    reshape x0 -> x1, local copies, waits for them, and re-layouts: none -> 6.6 us  [shards(): jnp.concatenate(lax.all_to_all(jnp.stack(jnp.split(mirror, lax.psum(1, ax...]
    all_to_all x2 -> x0, local copies, waits for them, and re-layouts: 5.85 us -> none  [shards(): lax.all_to_all(mirror, 'blk', split_axis=1, concat_axis=2, tiled=True)]
    another operation x0 -> x1, other arithmetic: none -> 2.96 us  [shards(): jnp.stack(jnp.split(mirror, lax.psum(1, axis_name='blk'), axis=1), axis=0)]
where the time goes in v1:
time: 272 us; the launch traced here: 271 us
  waiting for transfers between devices  100 us (37%)
  blocking collectives  65.4 us (24%)
  local copies, waits for them, and re-layouts  51.6 us (19%)
  matrix products  24.4 us (9%)
  between operations  16 us (6%)
  other arithmetic  11.2 us (4%)
  starting transfers between devices  2.74 us (1%)
    ppermute x1, waiting for transfers between devices, partner(): lax.ppermute(value, axis, [(i, i ^ 1 << apart) for i in range(lax.axis_si...  91 us
    all_to_all x1, blocking collectives, shards(): lax.all_to_all(combined, 'pair', split_axis=0, concat_axis=0, tiled=True)  57 us
    gather x1, local copies, waits for them, and re-layouts, shards(): picked = elementals[pairs[:, 0][:, None], elem_index]  19 us
    another operation x2, local copies, waits for them, and re-layouts, shards(): jnp.stack([dressed_real, dressed_imag]).astype(jnp.bfloat16)  10.7 us
    dot_general x1, matrix products, shards(): jnp.einsum('zrc,ycr->zy', dressed, mirror_rows, preferred_element_type=jn...  9.3 us
    all_gather x1, waiting for transfers between devices, shards(): gathered = lax.all_gather(blocks[:, None], 'blk', axis=1, tiled=True)  9.08 us
    reshape x1, local copies, waits for them, and re-layouts, shards(): shaped = gathered.reshape(2 * peers, NS, NS, 2, entries // NV, NV)  7.7 us
    reshape x1, local copies, waits for them, and re-layouts, shards(): jnp.concatenate(lax.all_to_all(jnp.stack(jnp.split(mirror, lax.psum(1, ax...  6.6 us
  transfers between devices with their start and end apart: 2, of which 2 were waited for; matrix products, arithmetic and copies ran while one was open for 1% of the time, Pallas kernels for 0%

profile of v1, /device:TPU:0, one launch (start us, length us, event | category | flops | bytes accessed | tf_op | source)
XLA Modules:
  0.0 271.4 jit_solution(1013394576069577573)
XLA Ops:
  8.9 19.0 %gather_fusion = bf16[384,2,2048]{2,1,0:T(2,128)(2,1)} fusion(bf16[16,8,2,2048]{3,2,1,0:T(2,128)(2,1)S(1)} %copy-done, s32[384]{0:T(512)S(1)} %reshape.52), kind=kCustom, calls=%fused_computation | custom fusion | bytes 6294528 | tf_op jit(solution)/shard_map/gather | solution.py:20
  28.0 4.5 %fusion.2 = bf16[16,4,4,2,2048]{4,2,3,1,0:T(4,128)(2,1)S(1)} fusion(bf16[16,24,2,2048,1]{3,2,1,0,4:T(2,128)(2,1)} %bitcast.97, s32[16,24,4,4]{1,3,2,0:T(4,128)S(1)} %copy-done.6, f32[16,24]{1,0:T(8,128)S(1)} %fusion.20), kind=kOutput, calls=%fused_computation.3 | convolution fusion | flops 51398656 | bytes 5268992 | tf_op jit(solution)/shard_map/pkab,pkcf->pabcf/dot_general | solution.py:21
  32.5 57.0 %all_to_all.10 = bf16[16,4,4,2,2048]{4,2,3,1,0:T(4,128)(2,1)} all-to-all(bf16[16,4,4,2,2048]{4,2,3,1,0:T(4,128)(2,1)S(1)} %fusion.2), channel_id=1, replica_groups=mesh['cfg'=1,'pair'=16,'blk'=2] {'pair'}, dimensions={0} | all-to-all | bytes 4194304 | tf_op jit(solution)/shard_map/all_to_all | solution.py:24
  89.5 1.6 copy-done.3
  91.1 1.5 fusion.24
  92.6 9.1 %all-gather.3.cloned.1.call-done = bf16[16,8,4,2,2048]{4,2,3,1,0:T(4,128)(2,1)} async-done(((bf16[16,4,4,2,2048]{4,2,3,1,0:T(4,128)(2,1)}), bf16[16,8,4,2,2048]{4,2,3,1,0:T(4,128)(2,1)}) %all-gather.3.cloned.1.call-update) | async-done | bytes 4194320 | tf_op jit(solution)/shard_map/all_gather | solution.py:25
  101.7 7.7 %reshape.49 = bf16[32,4,4,2,8,256]{5,4,2,3,1,0:T(8,128)(2,1)} reshape(bf16[16,8,4,2,2048]{4,2,3,1,0:T(4,128)(2,1)} %all-gather.3.cloned.1.call-done) | data formatting | bytes 8388608 | tf_op jit(solution)/shard_map/reshape | solution.py:28
  109.4 3.0 %fusion.7 = f32[32,4,8,512,1]{3,2,4,1,0:T(8,128)S(1)} fusion(bf16[4,256,512,1,1]{2,1,0,4,3:T(8,128)(2,1)S(1)} %bitcast.102, bf16[32,4,4,2,8,256]{5,4,2,3,1,0:T(8,128)(2,1)} %reshape.49), kind=kOutput, calls=%fused_computation.12 | convolution fusion | flops 1073741824 | bytes 5242880 | tf_op jit(solution)/shard_map/gabuj,bjn->agun/dot_general | solution.py:37
  112.5 2.6 fusion.8
  115.1 1.2 fusion.12
  116.3 1.1 copy.15
  117.4 4.7 %copy.17 = bf16[1,1024,512]{1,0,2:T(2,128)(2,1)S(1)} copy(bf16[1,1024,512]{2,1,0:T(8,128)(2,1)} %bitcast.99) | data formatting | bytes 2097152 | tf_op jit(solution)/shard_map/stack | solution.py:41
  122.2 3.8 %fusion.11 = bf16[4,32,8,512]{3,2,0,1:T(8,128)(2,1)S(1)} fusion(bf16[4,256,512,1,1]{2,1,0,4,3:T(8,128)(2,1)} %bitcast.101, bf16[32,4,4,2,8,256]{5,4,2,3,1,0:T(8,128)(2,1)} %reshape.49, f32[32,4,8,512,1]{3,2,4,1,0:T(8,128)} %fusion.8), kind=kOutput, calls=%fused_computation.16 | convolution fusion | flops 1074790400 | bytes 6291456 | tf_op jit(solution)/shard_map/gabuj,bjn->agun/dot_general | solution.py:36
  126.0 1.1 copy.14
  127.0 6.0 %copy.16 = bf16[1,1024,512]{1,0,2:T(2,128)(2,1)} copy(bf16[1,1024,512]{2,1,0:T(8,128)(2,1)} %bitcast.100) | data formatting | bytes 2097152 | tf_op jit(solution)/shard_map/stack | solution.py:41
  133.0 5.9 %pad_maximum_fusion = bf16[2,1024,512]{1,0,2:T(2,128)(2,1)S(1)} fusion(bf16[1,1024,512]{1,0,2:T(2,128)(2,1)S(1)} %copy.17, bf16[1,1024,512]{1,0,2:T(2,128)(2,1)} %copy.16), kind=kLoop, calls=%fused_computation.6 | loop fusion | flops 4194304 | bytes 4194304 | tf_op jit(solution)/shard_map/stack | solution.py:41
  138.9 2.7 %collective-permute-start = (bf16[2,1024,512]{1,0,2:T(2,128)(2,1)S(1)}, bf16[2,1024,512]{1,0,2:T(2,128)(2,1)S(1)}, u32[]{:S(2)}, u32[]{:S(2)}) collective-permute-start(bf16[2,1024,512]{1,0,2:T(2,128)(2,1)S(1)} %pad_maximum_fusion), channel_id=1, source_target_pairs={{0,16},{2,18},{4,20},{6,22},{8,24},{10,26},{12,28},{14,30},{16,0},... | collective-permute-start | bytes 6291464 | tf_op jit(solution)/shard_map/ppermute | solution.py:11
  141.7 91.0 %collective-permute-done = bf16[2,1024,512]{1,0,2:T(2,128)(2,1)S(1)} collective-permute-done((bf16[2,1024,512]{1,0,2:T(2,128)(2,1)S(1)}, bf16[2,1024,512]{1,0,2:T(2,128)(2,1)S(1)}, u32[]{:S(2)}, u32[]{:S(2)}) %collective-permute-start) | collective-permute-done | bytes 2097184 | tf_op jit(solution)/shard_map/ppermute | solution.py:11
  232.7 1.5 slice_bitcast_fusion.15
  234.1 3.0 %pad_maximum_fusion.1 = bf16[2,2,512,512]{2,1,3,0:T(2,128)(2,1)S(1)} fusion(bf16[1,2,512,512]{2,1,3,0:T(2,128)(2,1)S(1)} %get-tuple-element.6, bf16[1,2,512,512]{2,1,3,0:T(2,128)(2,1)S(1)} %get-tuple-element.5), kind=kLoop, calls=%fused_computation.7 | loop fusion | flops 1048576 | bytes 4194304 | tf_op jit(solution)/shard_map/stack | solution.py:47
  237.1 5.4 %all_to_all.11 = bf16[2,2,512,512]{2,1,3,0:T(2,128)(2,1)S(1)} all-to-all(bf16[2,2,512,512]{2,1,3,0:T(2,128)(2,1)S(1)} %pad_maximum_fusion.1), channel_id=1, replica_groups=mesh['cfg'=1,'pair'=16,'blk'=2] {'blk'}, dimensions={0} | all-to-all | bytes 4194304 | tf_op jit(solution)/shard_map/all_to_all | solution.py:46
  242.5 6.6 %copy.29 = bf16[2,512,1024]{2,0,1:T(2,128)(2,1)} copy(bf16[2,512,1024]{1,0,2:T(2,128)(2,1)S(1)} %bitcast.98) | data formatting | bytes 4194304 | tf_op jit(solution)/shard_map/reshape | solution.py:45
  249.1 9.3 %convolution_bitcast_fusion = f32[2,2]{1,0:T(2,128)S(1)} fusion(bf16[2,1024,512]{1,0,2:T(2,128)(2,1)} %copy-done.2, bf16[2,512,1024]{2,0,1:T(2,128)(2,1)} %copy.29), kind=kOutput, calls=%fused_computation.18 | convolution fusion | flops 4194304 | bytes 4194320 | tf_op jit(solution)/shard_map/zrc,ycr->zy/dot_general | solution.py:54
  261.6 2.9 %psum.7 = f32[1,2]{1,0:T(1,128)} all-reduce(f32[1,2]{1,0:T(1,128)S(1)} %maximum_bitcast_fusion), channel_id=1, replica_groups=mesh['cfg'=1,'pair'=16,'blk'=2] {'blk'}, use_global_device_ids=true, to_apply=%region_0.0 | all-reduce | flops 2 | bytes 16 | tf_op jit(solution)/shard_map/psum | solution.py:56
  (21 shorter events, 3.2 us)
Async XLA Ops:
  6.5 2.4 copy-start
  6.5 95.2 %all-gather.3.cloned.1.call-start = ((), (), s32[]{:S(2)}) async-start(), calls=%async_computation.2 | async-start | bytes 6291456 | tf_op jit(solution)/shard_map/all_gather | solution.py:25
  8.9 19.1 %copy-start.6 = (s32[16,24,4,4]{1,3,2,0:T(4,128)S(1)}, s32[16,24,4,4]{1,3,2,0:T(4,128)}, u32[]{:S(2)}) copy-start(s32[16,24,4,4]{1,3,2,0:T(4,128)} %param.10) | copy-start | bytes 73732
  89.5 1.6 copy-start.3
  92.6 16.8 %copy-start.4 = (bf16[1,1,1024,512]{3,2,1,0:T(8,128)(2,1)S(1)}, bf16[1,1,1024,512]{3,2,1,0:T(8,128)(2,1)}, u32[]{:S(2)}) copy-start(bf16[1,1,1024,512]{3,2,1,0:T(8,128)(2,1)} %get-tuple-element.7) | copy-start | bytes 3145732
  109.4 3.0 %copy-start.1 = (bf16[32,4,4,2,8,256]{5,4,2,3,1,0:T(8,128)(2,1)S(1)}, bf16[32,4,4,2,8,256]{5,4,2,3,1,0:T(8,128)(2,1)}, u32[]{:S(2)}) copy-start(bf16[32,4,4,2,8,256]{5,4,2,3,1,0:T(8,128)(2,1)} %reshape.49) | copy-start | bytes 12582916
  109.4 3.1 %copy-start.5 = (bf16[1,1,1024,512]{3,2,1,0:T(8,128)(2,1)S(1)}, bf16[1,1,1024,512]{3,2,1,0:T(8,128)(2,1)}, u32[]{:S(2)}) copy-start(bf16[1,1,1024,512]{3,2,1,0:T(8,128)(2,1)} %get-tuple-element.8) | copy-start | bytes 3145732
  138.9 2.8 %copy-start.2 = (bf16[2,1024,512]{1,0,2:T(2,128)(2,1)}, bf16[2,1024,512]{1,0,2:T(2,128)(2,1)S(1)}, u32[]{:S(2)}) copy-start(bf16[2,1024,512]{1,0,2:T(2,128)(2,1)S(1)} %pad_maximum_fusion) | copy-start | bytes 6291460
  138.9 93.8 %collective-permute-start = (bf16[2,1024,512]{1,0,2:T(2,128)(2,1)S(1)}, bf16[2,1024,512]{1,0,2:T(2,128)(2,1)S(1)}, u32[]{:S(2)}, u32[]{:S(2)}) collective-permute-start(bf16[2,1024,512]{1,0,2:T(2,128)(2,1)S(1)} %pad_maximum_fusion), channel_id=1, source_target_pairs={{0,16},{2,18},{4,20},{6,22},{8,24},{10,26},{12,28},{14,30},{16,0},... | collective-permute-start | bytes 6291464 | tf_op jit(solution)/shard_map/ppermute | solution.py:11
Sparse Core Ops, SparseCore 0:
  89.7 11.9 all-gather.2
